TPU v7x, 32 devices: a whole 2x2x4 slice. The times are simulated.
32 devices in a mesh: section: 2 (over y), design: 8 (over z, x), batch: 2 (over core).
Axes of the slice: x: 2, y: 2, z: 4, core: 2. Of those that a mesh axis runs over, the one named last changes fastest.
Arguments:
- samples: float32 [64, 4096], replicated, may hold values from -6 to 6
- order: int32 [4096], P('batch'), may hold values from 0 to 4095, each once
- design_points: bfloat16 [2, 64, 16384], P('section', None, 'design'), may hold values from -6 to 6
- weights: bfloat16 [2, 64, 16384], P('section', None, 'design'), may hold values from -2 to 2
- length_sq: float32 [2, 64], replicated, may hold values from 8 to 128
Outputs:
- moments: float32 [2, 4, 64, 1024], P('section', None, None, ('batch', 'design'))
Inputs may be any that keep to these rules, and one draw needn't show every extreme that they name: `order`: each sample index appears exactly once.
All inputs are finite; a program needn't handle non-finite values.
Results may differ from a plain program's by a relative error of at most 0.0037.
Values may be sent and summed in bfloat16 or wider, within the bound.
A program may use at most 64 MiB of HBM per device.

v0:
```python
import jax
import jax.numpy as jnp
from jax import lax
from jax.sharding import PartitionSpec as P

MICRO = 512


def passed_along(block, axis, distance):
    devices = range(lax.axis_size(axis))
    route = [(i - distance, i) for i in devices if i - distance in devices]
    return lax.ppermute(block, axis, route)


def local_sum(mean_in, var_in, points, squares, weight_rows, lengths):
    denom = lengths[:, None] + 2.0 * var_in
    offset = jnp.sum(mean_in * mean_in / denom, axis=0)
    log_scale = -0.5 * jnp.sum(jnp.log(1.0 + 2.0 * var_in / lengths[:, None]), axis=0)
    scaled = (mean_in / denom).astype(jnp.bfloat16)
    inverse = (1.0 / denom).astype(jnp.bfloat16)
    cross = lax.dot_general(
        scaled, points, (((0,), (0,)), ((), ())), preferred_element_type=jnp.float32
    )
    quad = lax.dot_general(
        inverse, squares, (((0,), (0,)), ((), ())), preferred_element_type=jnp.float32
    )
    kernel = jnp.exp(log_scale[:, None] - offset[:, None] + 2.0 * cross - quad).astype(jnp.bfloat16)
    return lax.dot_general(
        weight_rows, kernel, (((1,), (1,)), ((), ())), preferred_element_type=jnp.float32
    )


def square_of(points):
    wide = points.astype(jnp.float32)
    return (wide * wide).astype(jnp.bfloat16)


def shards(samples, order, design_points, weights, length_sq):
    section_index = lax.axis_index("section")
    is_first = section_index == 0
    points = design_points[0]
    weight_rows = weights[0]
    lengths = jnp.where(is_first, length_sq[0], length_sq[1])
    squares = square_of(points)
    feat = points.shape[0]
    half = feat // 2
    count = order.shape[0] // MICRO
    share = MICRO // lax.axis_size("design")
    column = lax.axis_index("design") * share

    def pick(turn):
        indices = order[turn * MICRO : (turn + 1) * MICRO]
        return jnp.take(samples, indices, axis=1)

    received = jnp.zeros((feat, MICRO), jnp.float32)
    zeros_rest = jnp.zeros((feat - half, MICRO), jnp.float32)
    firsts = []
    seconds = []
    for turn in range(count + 1):
        current = pick(min(turn, count - 1))
        earlier = pick(max(turn - 1, 0))
        moments_in = received
        later_mean = jnp.concatenate([moments_in[:half], earlier[half:]], axis=0)
        later_var = jnp.concatenate([moments_in[half:], zeros_rest], axis=0)
        mean_in = jnp.where(is_first, current, later_mean)
        var_in = jnp.where(is_first, 0.0, later_var)
        partial_sum = local_sum(mean_in, var_in, points, squares, weight_rows, lengths)
        summed = lax.psum(partial_sum, "design")
        layer_out = jnp.where(
            is_first,
            jnp.concatenate([summed[:half], jax.nn.softplus(summed[half:])], axis=0),
            summed,
        )
        received = passed_along(layer_out, "section", 1)
        block = lax.dynamic_slice_in_dim(layer_out, column, share, 1)
        if turn < count:
            firsts.append(block)
        if turn > 0:
            seconds.append(block)
    result = jnp.where(is_first, jnp.stack(firsts, axis=0), jnp.stack(seconds, axis=0))
    return result[None]


def solution(mesh):
    placed = (P(), P("batch"), P("section", None, "design"), P("section", None, "design"), P())
    return jax.shard_map(
        shards,
        mesh=mesh,
        in_specs=placed,
        out_specs=P("section", None, None, ("batch", "design")),
        check_vma=False,
    )
```

profile of v0, /device:TPU:0, one launch (start us, length us, event | category | flops | bytes accessed | tf_op | source)
XLA Modules:
  0.0 447.8 jit_solution(6106497824247773900)
XLA Ops:
  9.5 1.8 copy.6
  11.3 1.0 gather_fusion
  12.6 2.7 fusion.23
  16.1 4.4 fusion.9
  20.5 73.3 %all-reduce.11.cloned.1.call-done = f32[64,512]{1,0:T(8,128)} async-done(((f32[64,512]{1,0:T(8,128)}), f32[64,512]{1,0:T(8,128)}) %all-reduce.11.cloned.1.call-update) | async-done | bytes 131088 | tf_op jit(solution)/shard_map/psum | solution.py:68
  94.8 4.3 collective-permute-start
  99.1 1.0 gather_fusion.1
  100.3 1.3 collective-permute-done
  101.7 2.7 fusion.21
  104.5 4.4 fusion.8
  109.0 70.6 %all-reduce.13.cloned.1.call-done = f32[64,512]{1,0:T(8,128)} async-done(((f32[64,512]{1,0:T(8,128)}), f32[64,512]{1,0:T(8,128)}) %all-reduce.13.cloned.1.call-update) | async-done | bytes 131088 | tf_op jit(solution)/shard_map/psum | solution.py:68
  180.6 4.9 %collective-permute-start.1 = (f32[64,512]{1,0:T(8,128)S(1)}, f32[64,512]{1,0:T(8,128)}, u32[]{:S(2)}, u32[]{:S(2)}) collective-permute-start(f32[64,512]{1,0:T(8,128)S(1)} %maximum_select_fusion.2), channel_id=1, source_target_pairs={{0,16},{1,17},{2,18},{3,19},{4,20},{5,21},{6,22},{7,23},{8,24},{9,... | collective-permute-start | bytes 393224 | tf_op jit(solution)/shard_map/ppermute | solution.py:12
  188.4 2.7 fusion.19
  191.1 4.4 fusion.7
  195.6 70.7 %all-reduce.15.cloned.1.call-done = f32[64,512]{1,0:T(8,128)} async-done(((f32[64,512]{1,0:T(8,128)}), f32[64,512]{1,0:T(8,128)}) %all-reduce.15.cloned.1.call-update) | async-done | bytes 131088 | tf_op jit(solution)/shard_map/psum | solution.py:68
  267.3 4.9 %collective-permute-start.2 = (f32[64,512]{1,0:T(8,128)S(1)}, f32[64,512]{1,0:T(8,128)}, u32[]{:S(2)}, u32[]{:S(2)}) collective-permute-start(f32[64,512]{1,0:T(8,128)S(1)} %maximum_select_fusion.4), channel_id=1, source_target_pairs={{0,16},{1,17},{2,18},{3,19},{4,20},{5,21},{6,22},{7,23},{8,24},{9,... | collective-permute-start | bytes 393224 | tf_op jit(solution)/shard_map/ppermute | solution.py:12
  275.1 2.7 fusion.17
  277.8 4.4 fusion.6
  282.3 70.8 %all-reduce.17.cloned.1.call-done = f32[64,512]{1,0:T(8,128)} async-done(((f32[64,512]{1,0:T(8,128)}), f32[64,512]{1,0:T(8,128)}) %all-reduce.17.cloned.1.call-update) | async-done | bytes 131088 | tf_op jit(solution)/shard_map/psum | solution.py:68
  354.0 4.3 collective-permute-start.3
  358.5 2.3 collective-permute-done.3
  361.0 2.7 fusion.15
  363.7 4.4 fusion.5
  368.3 70.5 %all-reduce.19.cloned.1.call-done = f32[64,512]{1,0:T(8,128)} async-done(((f32[64,512]{1,0:T(8,128)}), f32[64,512]{1,0:T(8,128)}) %all-reduce.19.cloned.1.call-update) | async-done | bytes 131088 | tf_op jit(solution)/shard_map/psum | solution.py:68
  (62 shorter events, 16.1 us)
Async XLA Ops:
  6.5 9.5 %copy-start = (bf16[1,64,2048]{2,1,0:T(8,128)(2,1)S(1)}, bf16[1,64,2048]{2,1,0:T(8,128)(2,1)}, u32[]{:S(2)}) copy-start(bf16[1,64,2048]{2,1,0:T(8,128)(2,1)} %param.10) | copy-start | bytes 786436
  6.5 6.1 %copy-start.1 = (bf16[1,64,2048]{2,1,0:T(8,128)(2,1)S(1)}, bf16[1,64,2048]{2,1,0:T(8,128)(2,1)}, u32[]{:S(2)}) copy-start(bf16[1,64,2048]{2,1,0:T(8,128)(2,1)} %param.9) | copy-start | bytes 786436
  6.5 87.3 %all-reduce.11.cloned.1.call-start = ((), (), s32[]{:S(2)}) async-start(), calls=%async_computation | async-start | bytes 262144 | tf_op jit(solution)/shard_map/psum | solution.py:68
  20.5 159.1 %all-reduce.13.cloned.1.call-start = ((), (), s32[]{:S(2)}) async-start(), calls=%async_computation.1 | async-start | bytes 262144 | tf_op jit(solution)/shard_map/psum | solution.py:68
  94.8 6.8 %collective-permute-start = (f32[64,512]{1,0:T(8,128)S(1)}, f32[64,512]{1,0:T(8,128)S(1)}, u32[]{:S(2)}, u32[]{:S(2)}) collective-permute-start(f32[64,512]{1,0:T(8,128)S(1)} %maximum_select_fusion), channel_id=1, source_target_pairs={{0,16},{1,17},{2,18},{3,19},{4,20},{5,21},{6,22},{7,23},{8,24},{9,... | collective-permute-start | bytes 393224 | tf_op jit(solution)/shard_map/ppermute | solution.py:12
  108.9 157.4 %all-reduce.15.cloned.1.call-start = ((), (), s32[]{:S(2)}) async-start(), calls=%async_computation.2 | async-start | bytes 262144 | tf_op jit(solution)/shard_map/psum | solution.py:68
  180.6 6.8 %collective-permute-start.1 = (f32[64,512]{1,0:T(8,128)S(1)}, f32[64,512]{1,0:T(8,128)}, u32[]{:S(2)}, u32[]{:S(2)}) collective-permute-start(f32[64,512]{1,0:T(8,128)S(1)} %maximum_select_fusion.2), channel_id=1, source_target_pairs={{0,16},{1,17},{2,18},{3,19},{4,20},{5,21},{6,22},{7,23},{8,24},{9,... | collective-permute-start | bytes 393224 | tf_op jit(solution)/shard_map/ppermute | solution.py:12
  195.5 157.5 %all-reduce.17.cloned.1.call-start = ((), (), s32[]{:S(2)}) async-start(), calls=%async_computation.3 | async-start | bytes 262144 | tf_op jit(solution)/shard_map/psum | solution.py:68
  267.3 6.8 %collective-permute-start.2 = (f32[64,512]{1,0:T(8,128)S(1)}, f32[64,512]{1,0:T(8,128)}, u32[]{:S(2)}, u32[]{:S(2)}) collective-permute-start(f32[64,512]{1,0:T(8,128)S(1)} %maximum_select_fusion.4), channel_id=1, source_target_pairs={{0,16},{1,17},{2,18},{3,19},{4,20},{5,21},{6,22},{7,23},{8,24},{9,... | collective-permute-start | bytes 393224 | tf_op jit(solution)/shard_map/ppermute | solution.py:12
  282.3 156.6 %all-reduce.19.cloned.1.call-start = ((), (), s32[]{:S(2)}) async-start(), calls=%async_computation.4 | async-start | bytes 262144 | tf_op jit(solution)/shard_map/psum | solution.py:68
  354.0 6.8 %collective-permute-start.3 = (f32[64,512]{1,0:T(8,128)S(1)}, f32[64,512]{1,0:T(8,128)S(1)}, u32[]{:S(2)}, u32[]{:S(2)}) collective-permute-start(f32[64,512]{1,0:T(8,128)S(1)} %maximum_select_fusion.6), channel_id=1, source_target_pairs={{0,16},{1,17},{2,18},{3,19},{4,20},{5,21},{6,22},{7,23},{8,24},{9,... | collective-permute-start | bytes 393224 | tf_op jit(solution)/shard_map/ppermute | solution.py:12
Sparse Core Ops, SparseCore 0:
  20.6 73.1 all-reduce.10
  109.0 70.5 all-reduce.12
  195.7 70.6 all-reduce.14
  282.4 70.6 all-reduce.16
  368.3 70.5 all-reduce.18
where the time goes:
time: 449 us; the launch traced here: 448 us
  waiting for transfers between devices  361 us (80%)
  matrix products  35.7 us (8%)
  starting transfers between devices  18.6 us (4%)
  between operations  14 us (3%)
  other arithmetic  9.83 us (2%)
  local copies, waits for them, and re-layouts  8.53 us (2%)
    psum x5, waiting for transfers between devices, shards(): summed = lax.psum(partial_sum, 'design')  356 us
    dot_general x5, matrix products, local_sum(): lax.dot_general(weight_rows, kernel, (((1,), (1,)), ((), ())), preferred_...  22.1 us
    ppermute x4, starting transfers between devices, passed_along(): return lax.ppermute(block, axis, route)  18.4 us
    dot_general x5, matrix products, local_sum(): lax.dot_general(scaled, points, (((0,), (0,)), ((), ())), preferred_eleme...  13.6 us
  transfers between devices with their start and end apart: 9, of which 9 were waited for; matrix products, arithmetic and copies ran while one was open for 1% of the time, Pallas kernels for 0%

commit v1 on v0

--- a/solution.py
+++ b/solution.py
@@ -65,7 +65,7 @@
         mean_in = jnp.where(is_first, current, later_mean)
         var_in = jnp.where(is_first, 0.0, later_var)
         partial_sum = local_sum(mean_in, var_in, points, squares, weight_rows, lengths)
-        summed = lax.psum(partial_sum, "design")
+        summed = jnp.sum(lax.all_gather(partial_sum, "design"), axis=0)
         layer_out = jnp.where(
             is_first,
             jnp.concatenate([summed[:half], jax.nn.softplus(summed[half:])], axis=0),

time: 449 us -> 305 us (0.68)
  waiting for transfers between devices: 361 us -> 211 us
  other arithmetic: 9.83 us -> 16.4 us
    psum x5 -> x0, waiting for transfers between devices: 356 us -> none  [shards(): summed = lax.psum(partial_sum, 'design')]
    all_gather x0 -> x5, waiting for transfers between devices: none -> 201 us  [shards(): summed = jnp.sum(lax.all_gather(partial_sum, 'design'), axis=0)]
    reduce_sum x0 -> x5, other arithmetic: none -> 6.53 us  [shards(): summed = jnp.sum(lax.all_gather(partial_sum, 'design'), axis=0)]
    ppermute x4, waiting for transfers between devices: 5.04 us -> 10.1 us  [passed_along(): return lax.ppermute(block, axis, route)]
  transfers between devices with their start and end apart: 9 -> 9, of which waited for: 9 -> 9; matrix products, arithmetic and copies ran while one was open for 1% -> 2% of each run, Pallas kernels for 0% -> 0%
where the time goes in v1:
time: 305 us; the launch traced here: 304 us
  waiting for transfers between devices  211 us (69%)
  matrix products  35.2 us (12%)
  other arithmetic  16.4 us (5%)
  starting transfers between devices  14.6 us (5%)
  between operations  14.1 us (5%)
  local copies, waits for them, and re-layouts  12.8 us (4%)
    all_gather x5, waiting for transfers between devices, shards(): summed = jnp.sum(lax.all_gather(partial_sum, 'design'), axis=0)  201 us
    dot_general x5, matrix products, local_sum(): lax.dot_general(weight_rows, kernel, (((1,), (1,)), ((), ())), preferred_...  21.7 us
    ppermute x4, starting transfers between devices, passed_along(): return lax.ppermute(block, axis, route)  14.4 us
    dot_general x5, matrix products, local_sum(): lax.dot_general(scaled, points, (((0,), (0,)), ((), ())), preferred_eleme...  13.5 us
    ppermute x4, waiting for transfers between devices, passed_along(): return lax.ppermute(block, axis, route)  10.1 us
    reduce_sum x5, other arithmetic, shards(): summed = jnp.sum(lax.all_gather(partial_sum, 'design'), axis=0)  6.53 us
  transfers between devices with their start and end apart: 9, of which 9 were waited for; matrix products, arithmetic and copies ran while one was open for 2% of the time, Pallas kernels for 0%

profile of v1, /device:TPU:0, one launch (start us, length us, event | category | flops | bytes accessed | tf_op | source)
XLA Modules:
  0.0 304.3 jit_solution(6445253951246476393)
XLA Ops:
  9.5 1.8 copy.19
  13.0 2.7 fusion.23
  16.3 4.4 %fusion.5 = f32[64,512]{1,0:T(8,128)} fusion(f32[512,2048]{1,0:T(8,128)} %fusion.23, f32[512]{0:T(512)S(1)} %broadcast_subtract_fusion, bf16[1,64,2048]{2,1,0:T(8,128)(2,1)S(1)} %copy-done, bf16[1,64,2048]{2,1,0:T(8,128)(2,1)S(1)} %copy-done.1, bf16[64]{0:T(256)(128)(2,1)S(1)} %get-tuple-element.17), kind=kOutput, calls=%fused_computation.14 | convolution fusion | flops 273022976 | bytes 4851840 | tf_op jit(solution)/shard_map/dot_general | solution.py:28
  20.8 43.1 %all-gather.11.cloned.1.call-done = f32[512,512]{1,0:T(8,128)} async-done(((f32[64,512]{1,0:T(8,128)}), f32[512,512]{1,0:T(8,128)}) %all-gather.11.cloned.1.call-update) | async-done | bytes 1048592 | tf_op jit(solution)/shard_map/all_gather | solution.py:68
  65.7 3.4 %collective-permute-start = (f32[64,512]{0,1:T(8,128)S(1)}, f32[64,512]{0,1:T(8,128)S(1)}, u32[]{:S(2)}, u32[]{:S(2)}) collective-permute-start(f32[64,512]{0,1:T(8,128)S(1)} %maximum_select_fusion), channel_id=1, source_target_pairs={{0,16},{1,17},{2,18},{3,19},{4,20},{5,21},{6,22},{7,23},{8,24},{9,... | collective-permute-start | bytes 393224 | tf_op jit(solution)/shard_map/ppermute | solution.py:12
  69.2 1.6 gather_fusion.1
  70.8 2.2 collective-permute-done
  74.5 2.7 fusion.21
  77.2 4.3 %fusion.9 = f32[64,512]{1,0:T(8,128)} fusion(f32[512,2048]{1,0:T(8,128)} %fusion.21, f32[512]{0:T(512)S(1)} %multiply_subtract_fusion.3, bf16[1,64,2048]{2,1,0:T(8,128)(2,1)S(1)} %copy-done, bf16[1,64,2048]{2,1,0:T(8,128)(2,1)S(1)} %copy-done.1, f32[64]{0:T(128)S(1)} %get-tuple-element.18, f32[32,512]{0,1:T(8,128)S(1)} %get-tuple-element.32, pred[]{:T(512)S(6)} %eq.3), kind=kOutput, calls=%fused_computation.18 | convolution fusion | flops 273186816 | bytes 4917505 | tf_op jit(solution)/shard_map/dot_general | solution.py:28
  81.6 40.1 %all-gather.13.cloned.1.call-done = f32[512,512]{1,0:T(8,128)} async-done(((f32[64,512]{1,0:T(8,128)}), f32[512,512]{1,0:T(8,128)}) %all-gather.13.cloned.1.call-update) | async-done | bytes 1048592 | tf_op jit(solution)/shard_map/all_gather | solution.py:68
  123.5 4.1 %collective-permute-start.1 = (f32[64,512]{0,1:T(8,128)S(1)}, f32[64,512]{0,1:T(8,128)}, u32[]{:S(2)}, u32[]{:S(2)}) collective-permute-start(f32[64,512]{0,1:T(8,128)S(1)} %maximum_select_fusion.2), channel_id=1, source_target_pairs={{0,16},{1,17},{2,18},{3,19},{4,20},{5,21},{6,22},{7,23},{8,24},{9,... | collective-permute-start | bytes 393224 | tf_op jit(solution)/shard_map/ppermute | solution.py:12
  133.2 2.7 fusion.19
  135.9 4.3 %fusion.8 = f32[64,512]{1,0:T(8,128)} fusion(f32[512,2048]{1,0:T(8,128)} %fusion.19, f32[512]{0:T(512)S(1)} %multiply_subtract_fusion.2, bf16[1,64,2048]{2,1,0:T(8,128)(2,1)S(1)} %copy-done, bf16[1,64,2048]{2,1,0:T(8,128)(2,1)S(1)} %copy-done.1, f32[64]{0:T(128)S(1)} %get-tuple-element.18, f32[32,512]{0,1:T(8,128)S(1)} %get-tuple-element.28, pred[]{:T(512)S(6)} %eq.3), kind=kOutput, calls=%fused_computation.17 | convolution fusion | flops 273186816 | bytes 4917505 | tf_op jit(solution)/shard_map/dot_general | solution.py:28
  140.4 40.2 %all-gather.15.cloned.1.call-done = f32[512,512]{1,0:T(8,128)} async-done(((f32[64,512]{1,0:T(8,128)}), f32[512,512]{1,0:T(8,128)}) %all-gather.15.cloned.1.call-update) | async-done | bytes 1048592 | tf_op jit(solution)/shard_map/all_gather | solution.py:68
  183.1 3.6 %collective-permute-start.2 = (f32[64,512]{0,1:T(8,128)}, f32[64,512]{0,1:T(8,128)S(1)}, u32[]{:S(2)}, u32[]{:S(2)}) collective-permute-start(f32[64,512]{0,1:T(8,128)} %maximum_select_fusion.4), channel_id=1, source_target_pairs={{0,16},{1,17},{2,18},{3,19},{4,20},{5,21},{6,22},{7,23},{8,24},{9,... | collective-permute-start | bytes 393224 | tf_op jit(solution)/shard_map/ppermute | solution.py:12
  187.8 2.8 collective-permute-done.2
  191.2 2.7 fusion.17
  193.9 4.3 %fusion.7 = f32[64,512]{1,0:T(8,128)} fusion(f32[512,2048]{1,0:T(8,128)} %fusion.17, f32[512]{0:T(512)S(1)} %multiply_subtract_fusion.1, bf16[1,64,2048]{2,1,0:T(8,128)(2,1)S(1)} %copy-done, bf16[1,64,2048]{2,1,0:T(8,128)(2,1)S(1)} %copy-done.1, f32[64]{0:T(128)S(1)} %get-tuple-element.18, f32[32,512]{0,1:T(8,128)S(1)} %get-tuple-element.24, pred[]{:T(512)S(6)} %eq.3), kind=kOutput, calls=%fused_computation.16 | convolution fusion | flops 273186816 | bytes 4917505 | tf_op jit(solution)/shard_map/dot_general | solution.py:28
  198.3 40.0 %all-gather.17.cloned.1.call-done = f32[512,512]{1,0:T(8,128)} async-done(((f32[64,512]{1,0:T(8,128)}), f32[512,512]{1,0:T(8,128)}) %all-gather.17.cloned.1.call-update) | async-done | bytes 1048592 | tf_op jit(solution)/shard_map/all_gather | solution.py:68
  240.1 3.4 %collective-permute-start.3 = (f32[64,512]{0,1:T(8,128)S(1)}, f32[64,512]{0,1:T(8,128)S(1)}, u32[]{:S(2)}, u32[]{:S(2)}) collective-permute-start(f32[64,512]{0,1:T(8,128)S(1)} %maximum_select_fusion.6), channel_id=1, source_target_pairs={{0,16},{1,17},{2,18},{3,19},{4,20},{5,21},{6,22},{7,23},{8,24},{9,... | collective-permute-start | bytes 393224 | tf_op jit(solution)/shard_map/ppermute | solution.py:12
  243.6 3.7 %collective-permute-done.3 = f32[64,512]{0,1:T(8,128)S(1)} collective-permute-done((f32[64,512]{0,1:T(8,128)S(1)}, f32[64,512]{0,1:T(8,128)S(1)}, u32[]{:S(2)}, u32[]{:S(2)}) %collective-permute-start.3) | collective-permute-done | bytes 131104 | tf_op jit(solution)/shard_map/ppermute | solution.py:12
  247.8 2.7 fusion.15
  250.5 4.3 %fusion.6 = f32[64,512]{1,0:T(8,128)} fusion(f32[512,2048]{1,0:T(8,128)} %fusion.15, f32[512]{0:T(512)S(1)} %multiply_subtract_fusion, bf16[1,64,2048]{2,1,0:T(8,128)(2,1)S(1)} %copy-done, bf16[1,64,2048]{2,1,0:T(8,128)(2,1)S(1)} %copy-done.1, f32[64]{0:T(128)S(1)} %get-tuple-element.18, f32[32,512]{0,1:T(8,128)S(1)} %get-tuple-element.20, pred[]{:T(512)S(6)} %eq.3), kind=kOutput, calls=%fused_computation.15 | convolution fusion | flops 273186816 | bytes 4917505 | tf_op jit(solution)/shard_map/dot_general | solution.py:28
  257.5 37.5 %all-gather.19.cloned.1.call-done = f32[512,512]{1,0:T(8,128)} async-done(((f32[64,512]{1,0:T(8,128)}), f32[512,512]{1,0:T(8,128)}) %all-gather.19.cloned.1.call-update) | async-done | bytes 1048592 | tf_op jit(solution)/shard_map/all_gather | solution.py:68
  (83 shorter events, 27.4 us)
Async XLA Ops:
  6.5 9.8 %copy-start = (bf16[1,64,2048]{2,1,0:T(8,128)(2,1)S(1)}, bf16[1,64,2048]{2,1,0:T(8,128)(2,1)}, u32[]{:S(2)}) copy-start(bf16[1,64,2048]{2,1,0:T(8,128)(2,1)} %param.10) | copy-start | bytes 786436
  6.5 6.4 %copy-start.1 = (bf16[1,64,2048]{2,1,0:T(8,128)(2,1)S(1)}, bf16[1,64,2048]{2,1,0:T(8,128)(2,1)}, u32[]{:S(2)}) copy-start(bf16[1,64,2048]{2,1,0:T(8,128)(2,1)} %param.9) | copy-start | bytes 786436
  6.5 57.4 %all-gather.11.cloned.1.call-start = ((), (), s32[]{:S(2)}) async-start(), calls=%async_computation | async-start | bytes 1179648 | tf_op jit(solution)/shard_map/all_gather | solution.py:68
  20.8 100.9 %all-gather.13.cloned.1.call-start = ((), (), s32[]{:S(2)}) async-start(), calls=%async_computation.1 | async-start | bytes 1179648 | tf_op jit(solution)/shard_map/all_gather | solution.py:68
  65.7 5.1 %copy-start.2 = (f32[64,512]{0,1:T(8,128)}, f32[64,512]{0,1:T(8,128)S(1)}, u32[]{:S(2)}) copy-start(f32[64,512]{0,1:T(8,128)S(1)} %maximum_select_fusion) | copy-start | bytes 393220
  65.7 7.3 %collective-permute-start = (f32[64,512]{0,1:T(8,128)S(1)}, f32[64,512]{0,1:T(8,128)S(1)}, u32[]{:S(2)}, u32[]{:S(2)}) collective-permute-start(f32[64,512]{0,1:T(8,128)S(1)} %maximum_select_fusion), channel_id=1, source_target_pairs={{0,16},{1,17},{2,18},{3,19},{4,20},{5,21},{6,22},{7,23},{8,24},{9,... | collective-permute-start | bytes 393224 | tf_op jit(solution)/shard_map/ppermute | solution.py:12
  81.5 99.0 %all-gather.15.cloned.1.call-start = ((), (), s32[]{:S(2)}) async-start(), calls=%async_computation.2 | async-start | bytes 1179648 | tf_op jit(solution)/shard_map/all_gather | solution.py:68
  123.5 5.9 %copy-start.3 = (f32[64,512]{0,1:T(8,128)}, f32[64,512]{0,1:T(8,128)S(1)}, u32[]{:S(2)}) copy-start(f32[64,512]{0,1:T(8,128)S(1)} %maximum_select_fusion.2) | copy-start | bytes 393220
  123.5 7.3 %collective-permute-start.1 = (f32[64,512]{0,1:T(8,128)S(1)}, f32[64,512]{0,1:T(8,128)}, u32[]{:S(2)}, u32[]{:S(2)}) collective-permute-start(f32[64,512]{0,1:T(8,128)S(1)} %maximum_select_fusion.2), channel_id=1, source_target_pairs={{0,16},{1,17},{2,18},{3,19},{4,20},{5,21},{6,22},{7,23},{8,24},{9,... | collective-permute-start | bytes 393224 | tf_op jit(solution)/shard_map/ppermute | solution.py:12
  140.3 98.0 %all-gather.17.cloned.1.call-start = ((), (), s32[]{:S(2)}) async-start(), calls=%async_computation.3 | async-start | bytes 1179648 | tf_op jit(solution)/shard_map/all_gather | solution.py:68
  183.1 7.6 %collective-permute-start.2 = (f32[64,512]{0,1:T(8,128)}, f32[64,512]{0,1:T(8,128)S(1)}, u32[]{:S(2)}, u32[]{:S(2)}) collective-permute-start(f32[64,512]{0,1:T(8,128)} %maximum_select_fusion.4), channel_id=1, source_target_pairs={{0,16},{1,17},{2,18},{3,19},{4,20},{5,21},{6,22},{7,23},{8,24},{9,... | collective-permute-start | bytes 393224 | tf_op jit(solution)/shard_map/ppermute | solution.py:12
  198.2 96.8 %all-gather.19.cloned.1.call-start = ((), (), s32[]{:S(2)}) async-start(), calls=%async_computation.4 | async-start | bytes 1179648 | tf_op jit(solution)/shard_map/all_gather | solution.py:68
  240.1 7.3 %collective-permute-start.3 = (f32[64,512]{0,1:T(8,128)S(1)}, f32[64,512]{0,1:T(8,128)S(1)}, u32[]{:S(2)}, u32[]{:S(2)}) collective-permute-start(f32[64,512]{0,1:T(8,128)S(1)} %maximum_select_fusion.6), channel_id=1, source_target_pairs={{0,16},{1,17},{2,18},{3,19},{4,20},{5,21},{6,22},{7,23},{8,24},{9,... | collective-permute-start | bytes 393224 | tf_op jit(solution)/shard_map/ppermute | solution.py:12
Sparse Core Ops, SparseCore 0:
  20.9 42.9 all-gather.10
  81.6 39.9 all-gather.12
  140.4 40.0 all-gather.14
  198.3 39.8 all-gather.16
  255.0 39.9 all-gather.18
